TPU v7x, 512 devices: a whole 4x8x8 slice. The times are simulated.
512 devices in a mesh: cuts: 16 (over y, z_hi), slab: 32 (over x, z_lo, core).
Axes of the slice: x: 4, y: 8, z: 8 (z_hi: 2, z_lo: 4; z = z_hi * 4 + z_lo), core: 2. Of those that a mesh axis runs over, the one named last changes fastest.
Arguments:
- states: float32 [16, 64, 256, 128], P(None, 'slab', 'cuts'), may hold values from -4 to 4
- diffusivity: float32 [64, 256, 128], P('slab'), may hold values from 0.04 to 0.08
- coarse_gain: float32 [64, 256, 128], P('slab'), may hold values from 0.2 to 0.99
- read_block: int32 [16, 16, 2], replicated, may hold values from 0 to 63
- read_count: int32 [16, 16], replicated, may hold values from 0 to 2, as said below
Outputs:
- new_states: float32 [16, 64, 256, 128], P(None, 'slab', 'cuts')
- fetched_blocks: float32 [16, 16, 2, 64, 4, 128], P('cuts', None, None, 'slab')
Inputs may be any that keep to these rules, and one draw needn't show every extreme that they name: `read_block`: block ids count in units of 4 y rows. Slots of read_block at or beyond read_count[d, s] are not read. In every draw some slice d reads 2 blocks from every slice.
All inputs are finite; a program needn't handle non-finite values.
Results may differ from a plain program's by a relative error of at most 0.00002.
Values sent between devices are 32-bit elements; how exact they have to be, the bound alone decides.
No kernel may reach another device: no remote copies, remote signals or barrier semaphores. Data moves between devices by JAX's collectives and lax.ppermute only.
A program may use at most 64 MiB of HBM per device.

v0:
```python
import jax
import jax.numpy as jnp
from jax import lax
from jax.sharding import PartitionSpec as P

FINE = 8
BY = 4
courant = 0.45


def with_halo(block, sides, width):
    for axis, dim in sides:
        count = lax.axis_size(axis)
        forward = [(i, i + 1) for i in range(count - 1)]
        backward = [(target, source) for source, target in forward]
        low = lax.ppermute(
            lax.slice_in_dim(block, block.shape[dim] - width, None, axis=dim), axis, forward
        )
        high = lax.ppermute(lax.slice_in_dim(block, 0, width, axis=dim), axis, backward)
        block = jnp.concatenate([low, block, high], axis=dim)
    return block


def entering(value, axis, join, neutral):
    count, mine = (lax.axis_size(axis), lax.axis_index(axis))
    pieces = jax.tree.map(lambda part: lax.all_gather(part, axis), value)
    subtotal = jax.tree.map(
        lambda part, zero: jnp.full_like(part, 0) + jnp.asarray(zero, part.dtype), value, neutral
    )

    def turn(position, subtotal):
        longer = join(subtotal, jax.tree.map(lambda part: part[position], pieces))
        return jax.tree.map(lambda new, old: jnp.where(position < mine, new, old), longer, subtotal)

    return lax.fori_loop(0, count - 1, turn, subtotal)


def face_values(kappa_ext):
    face_z = 0.5 * (kappa_ext[1:] + kappa_ext[:-1])
    pad_y = jnp.pad(kappa_ext, ((0, 0), (1, 1), (0, 0)))
    face_y = 0.5 * (pad_y[:, 1:] + pad_y[:, :-1])
    pad_x = jnp.pad(kappa_ext, ((0, 0), (0, 0), (1, 1)))
    face_x = 0.5 * (pad_x[:, :, 1:] + pad_x[:, :, :-1])
    return (face_z, face_y, face_x)


def fine_step(field, face_z, face_y, face_x):
    centre = field[1:-1]
    upper_z = field[2:]
    lower_z = field[:-2]
    flux_sum = face_z[1:] * (upper_z - centre) + face_z[:-1] * (lower_z - centre)
    pad_y = jnp.pad(centre, ((0, 0), (1, 1), (0, 0)))
    faces_y = face_y[1:-1]
    flux_sum = (
        flux_sum
        + faces_y[:, 1:] * (pad_y[:, 2:] - centre)
        + faces_y[:, :-1] * (pad_y[:, :-2] - centre)
    )
    pad_x = jnp.pad(centre, ((0, 0), (0, 0), (1, 1)))
    faces_x = face_x[1:-1]
    flux_sum = (
        flux_sum
        + faces_x[:, :, 1:] * (pad_x[:, :, 2:] - centre)
        + faces_x[:, :, :-1] * (pad_x[:, :, :-2] - centre)
    )
    return centre + flux_sum - courant * (centre - lower_z)


def combine(earlier, later):
    return (earlier[0] * later[0], later[0] * earlier[1] + later[1])


def body(states, diffusivity, coarse_gain, read_block, read_count):
    position = lax.axis_index("cuts")
    layers = diffusivity.shape[0]
    y_rows = diffusivity.shape[1]
    slice_start = lax.all_to_all(states, "cuts", split_axis=0, concat_axis=2, tiled=True)[0]
    halo_depth = 1
    kappa_ext = with_halo(diffusivity, (("slab", 0),), halo_depth)
    face_z, face_y, face_x = face_values(kappa_ext)

    def single_step(step_index, current):
        padded = with_halo(current, (("slab", 0),), 1)
        return fine_step(padded, face_z, face_y, face_x)

    fine_end = lax.fori_loop(0, FINE, single_step, slice_start)
    difference = fine_end - coarse_gain * slice_start
    blocks = fine_end.reshape(layers, y_rows // BY, BY, fine_end.shape[2]).transpose(1, 0, 2, 3)
    wanted_blocks = lax.dynamic_index_in_dim(read_block, position, 1, keepdims=False)
    counts = lax.dynamic_index_in_dim(read_count, position, 1, keepdims=False)
    picked = jnp.take(blocks, wanted_blocks, axis=0)
    live_slot = jnp.arange(read_block.shape[2], dtype=jnp.int32)[None, :] < counts[:, None]
    picked = jnp.where(live_slot[:, :, None, None, None], picked, 0.0)
    received = lax.all_to_all(picked, "cuts", split_axis=0, concat_axis=0, tiled=True)
    fetched_blocks = received[None]
    leading = position == 0
    factor = jnp.where(leading, 0.0, coarse_gain)
    offset = jnp.where(leading, difference + coarse_gain * slice_start, difference)
    identity = (jnp.ones_like(factor), jnp.zeros_like(offset))
    prefix_pair = entering((factor, offset), "cuts", combine, identity)
    newest = factor * prefix_pair[1] + offset
    new_states = lax.all_to_all(newest[None], "cuts", split_axis=2, concat_axis=0, tiled=True)
    return (new_states, fetched_blocks)


def solution(mesh):
    placed = (P(None, "slab", "cuts", None), P("slab", None, None), P("slab", None, None), P(), P())
    return jax.shard_map(
        body,
        mesh=mesh,
        in_specs=placed,
        out_specs=(P(None, "slab", "cuts", None), P("cuts", None, None, "slab", None, None)),
        check_vma=False,
    )
```

profile of v0, /device:TPU:2, one launch (start us, length us, event | category | flops | bytes accessed | tf_op | source)
XLA Modules:
  0.0 444.3 jit_solution(2078087062163330457)
XLA Ops:
  7.2 1.0 fusion.22
  8.2 1.9 collective-permute-start.3
  10.1 15.7 %all-to-all-start = ((f32[16,2,16,128]{3,2,1,0:T(8,128)}), f32[16,2,16,128]{3,2,1,0:T(8,128)S(1)}, u32[]{:S(2)}, u32[]{:S(2)}) async-start(f32[16,2,16,128]{3,2,1,0:T(8,128)} %param.9), calls=%async_computation | async-start | bytes 524288 | tf_op jit(solution)/shard_map/all_to_all | solution.py:77
  25.8 6.1 %collective-permute-start.2 = (f32[1,256,128]{2,1,0:T(8,128)S(1)}, f32[1,256,128]{2,1,0:T(8,128)S(1)}, u32[]{:S(2)}, u32[]{:S(2)}) collective-permute-start(f32[1,256,128]{2,1,0:T(8,128)S(1)} %get-tuple-element.210), channel_id=1, source_target_pairs={{1,0},{2,1},{3,2},{4,3},{5,4},{6,5},{7,6},{8,7},{9,8},{10,9},{11,1... | collective-permute-start | bytes 393224 | tf_op jit(solution)/shard_map/ppermute | solution.py:19
  31.9 1.0 constant_dynamic-update-slice_fusion.1
  32.9 3.4 collective-permute-done.2
  36.3 1.1 fusion.20
  37.9 4.8 %all-to-all-done = f32[16,2,16,128]{3,2,1,0:T(8,128)S(1)} async-done(((f32[16,2,16,128]{3,2,1,0:T(8,128)}), f32[16,2,16,128]{3,2,1,0:T(8,128)S(1)}, u32[]{:S(2)}, u32[]{:S(2)}) %all-to-all-start) | async-done | bytes 262176 | tf_op jit(solution)/shard_map/all_to_all | solution.py:77
  42.7 91.9 %while.26 = (s32[]{:T(128)}, f32[2,256,128]{2,1,0:T(8,128)S(1)}, f32[3,256,128]{2,1,0:T(8,128)S(1)}, f32[4,257,128]{2,1,0:T(8,128)S(1)}, f32[4,256,129]{2,1,0:T(8,128)S(1)}, /*index=5*/s32[]{:T(128)}) while((s32[]{:T(128)}, f32[2,256,128]{2,1,0:T(8,128)S(1)}, f32[3,256,128]{2,1,0:T(8,128)S(1)}, f32[4,257,128]{2,1,0:T(8,128)S(1)}, ...), condition=%wide.region_1.2_spmd, body=%wide.region_0.1_spmd.sunk | while | flops 1507330 | bytes 4456597 | solution.py:86
  42.8 2.7 collective-permute-start
  45.5 5.7 %collective-permute-start.1 = (f32[1,256,128]{2,1,0:T(8,128)S(1)}, f32[1,256,128]{2,1,0:T(8,128)S(1)}, u32[]{:S(2)}, u32[]{:S(2)}) collective-permute-start(f32[1,256,128]{2,1,0:T(8,128)S(1)} %get-tuple-element.271), channel_id=1, source_target_pairs={{1,0},{2,1},{3,2},{4,3},{5,4},{6,5},{7,6},{8,7},{9,8},{10,9},{11,1... | collective-permute-start | bytes 393224 | tf_op jit(solution)/shard_map/while/body/eval_jaxpr/ppermute | solution.py:19
  51.2 0.8 collective-permute-done
  51.9 1.7 collective-permute-done.1
  54.0 1.9 collective-permute-start
  56.0 6.5 %collective-permute-start.1 = (f32[1,256,128]{2,1,0:T(8,128)S(1)}, f32[1,256,128]{2,1,0:T(8,128)S(1)}, u32[]{:S(2)}, u32[]{:S(2)}) collective-permute-start(f32[1,256,128]{2,1,0:T(8,128)S(1)} %get-tuple-element.271), channel_id=1, source_target_pairs={{1,0},{2,1},{3,2},{4,3},{5,4},{6,5},{7,6},{8,7},{9,8},{10,9},{11,1... | collective-permute-start | bytes 393224 | tf_op jit(solution)/shard_map/while/body/eval_jaxpr/ppermute | solution.py:19
  62.5 0.8 collective-permute-done
  63.3 1.7 collective-permute-done.1
  65.4 1.9 collective-permute-start
  67.3 6.5 %collective-permute-start.1 = (f32[1,256,128]{2,1,0:T(8,128)S(1)}, f32[1,256,128]{2,1,0:T(8,128)S(1)}, u32[]{:S(2)}, u32[]{:S(2)}) collective-permute-start(f32[1,256,128]{2,1,0:T(8,128)S(1)} %get-tuple-element.271), channel_id=1, source_target_pairs={{1,0},{2,1},{3,2},{4,3},{5,4},{6,5},{7,6},{8,7},{9,8},{10,9},{11,1... | collective-permute-start | bytes 393224 | tf_op jit(solution)/shard_map/while/body/eval_jaxpr/ppermute | solution.py:19
  73.8 0.8 collective-permute-done
  74.6 2.0 collective-permute-done.1
  77.0 1.9 collective-permute-start
  78.9 6.6 %collective-permute-start.1 = (f32[1,256,128]{2,1,0:T(8,128)S(1)}, f32[1,256,128]{2,1,0:T(8,128)S(1)}, u32[]{:S(2)}, u32[]{:S(2)}) collective-permute-start(f32[1,256,128]{2,1,0:T(8,128)S(1)} %get-tuple-element.271), channel_id=1, source_target_pairs={{1,0},{2,1},{3,2},{4,3},{5,4},{6,5},{7,6},{8,7},{9,8},{10,9},{11,1... | collective-permute-start | bytes 393224 | tf_op jit(solution)/shard_map/while/body/eval_jaxpr/ppermute | solution.py:19
  86.2 1.8 collective-permute-done.1
  88.4 1.9 collective-permute-start
  90.3 6.5 %collective-permute-start.1 = (f32[1,256,128]{2,1,0:T(8,128)S(1)}, f32[1,256,128]{2,1,0:T(8,128)S(1)}, u32[]{:S(2)}, u32[]{:S(2)}) collective-permute-start(f32[1,256,128]{2,1,0:T(8,128)S(1)} %get-tuple-element.271), channel_id=1, source_target_pairs={{1,0},{2,1},{3,2},{4,3},{5,4},{6,5},{7,6},{8,7},{9,8},{10,9},{11,1... | collective-permute-start | bytes 393224 | tf_op jit(solution)/shard_map/while/body/eval_jaxpr/ppermute | solution.py:19
  96.8 0.8 collective-permute-done
  97.6 2.6 collective-permute-done.1
  100.6 1.9 collective-permute-start
  102.5 6.6 %collective-permute-start.1 = (f32[1,256,128]{2,1,0:T(8,128)S(1)}, f32[1,256,128]{2,1,0:T(8,128)S(1)}, u32[]{:S(2)}, u32[]{:S(2)}) collective-permute-start(f32[1,256,128]{2,1,0:T(8,128)S(1)} %get-tuple-element.271), channel_id=1, source_target_pairs={{1,0},{2,1},{3,2},{4,3},{5,4},{6,5},{7,6},{8,7},{9,8},{10,9},{11,1... | collective-permute-start | bytes 393224 | tf_op jit(solution)/shard_map/while/body/eval_jaxpr/ppermute | solution.py:19
  109.8 1.8 collective-permute-done.1
  112.0 1.9 collective-permute-start
  113.9 6.6 %collective-permute-start.1 = (f32[1,256,128]{2,1,0:T(8,128)S(1)}, f32[1,256,128]{2,1,0:T(8,128)S(1)}, u32[]{:S(2)}, u32[]{:S(2)}) collective-permute-start(f32[1,256,128]{2,1,0:T(8,128)S(1)} %get-tuple-element.271), channel_id=1, source_target_pairs={{1,0},{2,1},{3,2},{4,3},{5,4},{6,5},{7,6},{8,7},{9,8},{10,9},{11,1... | collective-permute-start | bytes 393224 | tf_op jit(solution)/shard_map/while/body/eval_jaxpr/ppermute | solution.py:19
  120.5 0.8 collective-permute-done
  121.3 1.7 collective-permute-done.1
  123.4 1.9 collective-permute-start
  125.3 6.5 %collective-permute-start.1 = (f32[1,256,128]{2,1,0:T(8,128)S(1)}, f32[1,256,128]{2,1,0:T(8,128)S(1)}, u32[]{:S(2)}, u32[]{:S(2)}) collective-permute-start(f32[1,256,128]{2,1,0:T(8,128)S(1)} %get-tuple-element.271), channel_id=1, source_target_pairs={{1,0},{2,1},{3,2},{4,3},{5,4},{6,5},{7,6},{8,7},{9,8},{10,9},{11,1... | collective-permute-start | bytes 393224 | tf_op jit(solution)/shard_map/while/body/eval_jaxpr/ppermute | solution.py:19
  131.8 0.8 collective-permute-done
  132.6 1.7 collective-permute-done.1
  134.6 0.8 broadcast_select_fusion
  137.7 0.8 select_select_fusion
  138.5 6.1 %all-to-all-start.2 = ((f32[16,2,2,4,128]{4,3,2,1,0:T(4,128)}), f32[16,2,2,4,128]{4,3,2,1,0:T(4,128)S(1)}, u32[]{:S(2)}, u32[]{:S(2)}) async-start(f32[16,2,2,4,128]{4,3,2,1,0:T(4,128)} %select_select_fusion), calls=%async_computation.2 | async-start | bytes 262144 | tf_op jit(solution)/shard_map/all_to_all | solution.py:94
  144.6 121.9 %all-gather.5.cloned.1.call-done = f32[32,256,128]{2,1,0:T(8,128)} async-done(((f32[2,256,128]{2,1,0:T(8,128)}), f32[32,256,128]{2,1,0:T(8,128)}) %all-gather.5.cloned.1.call-update) | async-done | bytes 4194320 | tf_op jit(solution)/shard_map/all_gather | solution.py:26
  266.4 130.4 %all-gather.7.cloned.1.call-done = f32[32,256,128]{2,1,0:T(8,128)} async-done(((f32[2,256,128]{2,1,0:T(8,128)}), f32[32,256,128]{2,1,0:T(8,128)}) %all-gather.7.cloned.1.call-update) | async-done | bytes 4194320 | tf_op jit(solution)/shard_map/all_gather | solution.py:26
  396.8 19.1 %while.27 = (s32[]{:T(128)}, f32[2,256,128]{2,1,0:T(8,128)S(1)}, s32[]{:T(128)}, f32[16,2,256,128]{3,2,1,0:T(8,128)}, f32[16,2,256,128]{3,2,1,0:T(8,128)}, /*index=5*/s32[]{:T(128)}, s32[]{:T(128)}) while((s32[]{:T(128)}, f32[2,256,128]{2,1,0:T(8,128)S(1)}, s32[]{:T(128)}, f32[16,2,256,128]{3,2,1,0:T(8,128)}, ...), condition=%wide.region_3.4_spmd.clone, body=%wide.region_2.3_spmd.clone.sunk | while | flops 262148 | bytes 1048685 | solution.py:35
  396.8 1.2 fusion.28
  398.1 1.2 fusion.28
  399.3 1.2 fusion.28
  400.6 1.2 fusion.28
  401.9 1.2 fusion.28
  403.2 1.2 fusion.28
  404.4 1.2 fusion.28
  405.7 1.2 fusion.28
  407.0 1.2 fusion.28
  408.2 1.2 fusion.28
  409.5 1.2 fusion.28
  410.8 1.2 fusion.28
  412.1 1.2 fusion.28
  413.3 1.2 fusion.28
  414.6 1.2 fusion.28
  415.9 0.9 copy.19
  416.8 4.4 all-to-all-start.1
  421.3 14.8 %all-to-all-done.1 = f32[1,2,256,128]{3,1,0,2:T(2,128)S(1)} async-done(((f32[1,2,256,128]{3,1,0,2:T(2,128)}), f32[1,2,256,128]{3,1,0,2:T(2,128)S(1)}, u32[]{:S(2)}, u32[]{:S(2)}) %all-to-all-start.1) | async-done | bytes 262176 | tf_op jit(solution)/shard_map/all_to_all | solution.py:102
  436.1 0.7 copy.25
  (63 shorter events, 7.5 us)
Async XLA Ops:
  7.2 129.1 %copy-start = (s32[16,16,2]{1,2,0:T(2,128)S(1)}, s32[16,16,2]{1,2,0:T(2,128)}, u32[]{:S(2)}) copy-start(s32[16,16,2]{1,2,0:T(2,128)} %param.12) | copy-start | bytes 6148
  8.2 23.7 %collective-permute-start.3 = (f32[1,256,128]{2,1,0:T(8,128)S(1)}, f32[1,256,128]{2,1,0:T(8,128)S(1)}, u32[]{:S(2)}, u32[]{:S(2)}) collective-permute-start(f32[1,256,128]{2,1,0:T(8,128)S(1)} %get-tuple-element.209), channel_id=1, source_target_pairs={{0,1},{1,2},{2,3},{3,4},{4,5},{5,6},{6,7},{7,8},{8,9},{9,10},{10,1... | collective-permute-start | bytes 393224 | tf_op jit(solution)/shard_map/ppermute | solution.py:16
  10.1 32.5 %all-to-all-start = ((f32[16,2,16,128]{3,2,1,0:T(8,128)}), f32[16,2,16,128]{3,2,1,0:T(8,128)S(1)}, u32[]{:S(2)}, u32[]{:S(2)}) async-start(f32[16,2,16,128]{3,2,1,0:T(8,128)} %param.9), calls=%async_computation | async-start | bytes 524288 | tf_op jit(solution)/shard_map/all_to_all | solution.py:77
  25.8 240.7 %all-gather.5.cloned.1.call-start = ((), (), s32[]{:S(2)}) async-start(), calls=%async_computation.3 | async-start | bytes 4456448 | tf_op jit(solution)/shard_map/all_gather | solution.py:26
  25.8 10.5 %collective-permute-start.2 = (f32[1,256,128]{2,1,0:T(8,128)S(1)}, f32[1,256,128]{2,1,0:T(8,128)S(1)}, u32[]{:S(2)}, u32[]{:S(2)}) collective-permute-start(f32[1,256,128]{2,1,0:T(8,128)S(1)} %get-tuple-element.210), channel_id=1, source_target_pairs={{1,0},{2,1},{3,2},{4,3},{5,4},{6,5},{7,6},{8,7},{9,8},{10,9},{11,1... | collective-permute-start | bytes 393224 | tf_op jit(solution)/shard_map/ppermute | solution.py:19
  42.7 92.0 %copy-start.3 = (f32[2,256,128]{2,1,0:T(8,128)S(1)}, f32[2,256,128]{2,1,0:T(8,128)}, u32[]{:S(2)}) copy-start(f32[2,256,128]{2,1,0:T(8,128)} %param.11) | copy-start | bytes 786436
  42.7 94.1 %copy-start.4 = (s32[16,16]{1,0:T(8,128)S(1)}, s32[16,16]{1,0:T(8,128)}, u32[]{:S(2)}) copy-start(s32[16,16]{1,0:T(8,128)} %param.13) | copy-start | bytes 3076
  42.8 9.2 %collective-permute-start = (f32[1,256,128]{2,1,0:T(8,128)S(1)}, f32[1,256,128]{2,1,0:T(8,128)S(1)}, u32[]{:S(2)}, u32[]{:S(2)}) collective-permute-start(f32[1,256,128]{2,1,0:T(8,128)S(1)} %get-tuple-element.270), channel_id=1, source_target_pairs={{0,1},{1,2},{2,3},{3,4},{4,5},{5,6},{6,7},{7,8},{8,9},{9,10},{10,1... | collective-permute-start | bytes 393224 | tf_op jit(solution)/shard_map/while/body/eval_jaxpr/ppermute | solution.py:16
  45.5 8.2 %collective-permute-start.1 = (f32[1,256,128]{2,1,0:T(8,128)S(1)}, f32[1,256,128]{2,1,0:T(8,128)S(1)}, u32[]{:S(2)}, u32[]{:S(2)}) collective-permute-start(f32[1,256,128]{2,1,0:T(8,128)S(1)} %get-tuple-element.271), channel_id=1, source_target_pairs={{1,0},{2,1},{3,2},{4,3},{5,4},{6,5},{7,6},{8,7},{9,8},{10,9},{11,1... | collective-permute-start | bytes 393224 | tf_op jit(solution)/shard_map/while/body/eval_jaxpr/ppermute | solution.py:19
  54.0 9.2 %collective-permute-start = (f32[1,256,128]{2,1,0:T(8,128)S(1)}, f32[1,256,128]{2,1,0:T(8,128)S(1)}, u32[]{:S(2)}, u32[]{:S(2)}) collective-permute-start(f32[1,256,128]{2,1,0:T(8,128)S(1)} %get-tuple-element.270), channel_id=1, source_target_pairs={{0,1},{1,2},{2,3},{3,4},{4,5},{5,6},{6,7},{7,8},{8,9},{9,10},{10,1... | collective-permute-start | bytes 393224 | tf_op jit(solution)/shard_map/while/body/eval_jaxpr/ppermute | solution.py:16
  56.0 9.0 %collective-permute-start.1 = (f32[1,256,128]{2,1,0:T(8,128)S(1)}, f32[1,256,128]{2,1,0:T(8,128)S(1)}, u32[]{:S(2)}, u32[]{:S(2)}) collective-permute-start(f32[1,256,128]{2,1,0:T(8,128)S(1)} %get-tuple-element.271), channel_id=1, source_target_pairs={{1,0},{2,1},{3,2},{4,3},{5,4},{6,5},{7,6},{8,7},{9,8},{10,9},{11,1... | collective-permute-start | bytes 393224 | tf_op jit(solution)/shard_map/while/body/eval_jaxpr/ppermute | solution.py:19
  65.4 9.3 %collective-permute-start = (f32[1,256,128]{2,1,0:T(8,128)S(1)}, f32[1,256,128]{2,1,0:T(8,128)S(1)}, u32[]{:S(2)}, u32[]{:S(2)}) collective-permute-start(f32[1,256,128]{2,1,0:T(8,128)S(1)} %get-tuple-element.270), channel_id=1, source_target_pairs={{0,1},{1,2},{2,3},{3,4},{4,5},{5,6},{6,7},{7,8},{8,9},{9,10},{10,1... | collective-permute-start | bytes 393224 | tf_op jit(solution)/shard_map/while/body/eval_jaxpr/ppermute | solution.py:16
  67.3 9.3 %collective-permute-start.1 = (f32[1,256,128]{2,1,0:T(8,128)S(1)}, f32[1,256,128]{2,1,0:T(8,128)S(1)}, u32[]{:S(2)}, u32[]{:S(2)}) collective-permute-start(f32[1,256,128]{2,1,0:T(8,128)S(1)} %get-tuple-element.271), channel_id=1, source_target_pairs={{1,0},{2,1},{3,2},{4,3},{5,4},{6,5},{7,6},{8,7},{9,8},{10,9},{11,1... | collective-permute-start | bytes 393224 | tf_op jit(solution)/shard_map/while/body/eval_jaxpr/ppermute | solution.py:19
  77.0 9.2 %collective-permute-start = (f32[1,256,128]{2,1,0:T(8,128)S(1)}, f32[1,256,128]{2,1,0:T(8,128)S(1)}, u32[]{:S(2)}, u32[]{:S(2)}) collective-permute-start(f32[1,256,128]{2,1,0:T(8,128)S(1)} %get-tuple-element.270), channel_id=1, source_target_pairs={{0,1},{1,2},{2,3},{3,4},{4,5},{5,6},{6,7},{7,8},{8,9},{9,10},{10,1... | collective-permute-start | bytes 393224 | tf_op jit(solution)/shard_map/while/body/eval_jaxpr/ppermute | solution.py:16
  78.9 9.1 %collective-permute-start.1 = (f32[1,256,128]{2,1,0:T(8,128)S(1)}, f32[1,256,128]{2,1,0:T(8,128)S(1)}, u32[]{:S(2)}, u32[]{:S(2)}) collective-permute-start(f32[1,256,128]{2,1,0:T(8,128)S(1)} %get-tuple-element.271), channel_id=1, source_target_pairs={{1,0},{2,1},{3,2},{4,3},{5,4},{6,5},{7,6},{8,7},{9,8},{10,9},{11,1... | collective-permute-start | bytes 393224 | tf_op jit(solution)/shard_map/while/body/eval_jaxpr/ppermute | solution.py:19
  88.4 9.2 %collective-permute-start = (f32[1,256,128]{2,1,0:T(8,128)S(1)}, f32[1,256,128]{2,1,0:T(8,128)S(1)}, u32[]{:S(2)}, u32[]{:S(2)}) collective-permute-start(f32[1,256,128]{2,1,0:T(8,128)S(1)} %get-tuple-element.270), channel_id=1, source_target_pairs={{0,1},{1,2},{2,3},{3,4},{4,5},{5,6},{6,7},{7,8},{8,9},{9,10},{10,1... | collective-permute-start | bytes 393224 | tf_op jit(solution)/shard_map/while/body/eval_jaxpr/ppermute | solution.py:16
  90.3 9.9 %collective-permute-start.1 = (f32[1,256,128]{2,1,0:T(8,128)S(1)}, f32[1,256,128]{2,1,0:T(8,128)S(1)}, u32[]{:S(2)}, u32[]{:S(2)}) collective-permute-start(f32[1,256,128]{2,1,0:T(8,128)S(1)} %get-tuple-element.271), channel_id=1, source_target_pairs={{1,0},{2,1},{3,2},{4,3},{5,4},{6,5},{7,6},{8,7},{9,8},{10,9},{11,1... | collective-permute-start | bytes 393224 | tf_op jit(solution)/shard_map/while/body/eval_jaxpr/ppermute | solution.py:19
  100.6 9.3 %collective-permute-start = (f32[1,256,128]{2,1,0:T(8,128)S(1)}, f32[1,256,128]{2,1,0:T(8,128)S(1)}, u32[]{:S(2)}, u32[]{:S(2)}) collective-permute-start(f32[1,256,128]{2,1,0:T(8,128)S(1)} %get-tuple-element.270), channel_id=1, source_target_pairs={{0,1},{1,2},{2,3},{3,4},{4,5},{5,6},{6,7},{7,8},{8,9},{9,10},{10,1... | collective-permute-start | bytes 393224 | tf_op jit(solution)/shard_map/while/body/eval_jaxpr/ppermute | solution.py:16
  102.5 9.1 %collective-permute-start.1 = (f32[1,256,128]{2,1,0:T(8,128)S(1)}, f32[1,256,128]{2,1,0:T(8,128)S(1)}, u32[]{:S(2)}, u32[]{:S(2)}) collective-permute-start(f32[1,256,128]{2,1,0:T(8,128)S(1)} %get-tuple-element.271), channel_id=1, source_target_pairs={{1,0},{2,1},{3,2},{4,3},{5,4},{6,5},{7,6},{8,7},{9,8},{10,9},{11,1... | collective-permute-start | bytes 393224 | tf_op jit(solution)/shard_map/while/body/eval_jaxpr/ppermute | solution.py:19
  112.0 9.3 %collective-permute-start = (f32[1,256,128]{2,1,0:T(8,128)S(1)}, f32[1,256,128]{2,1,0:T(8,128)S(1)}, u32[]{:S(2)}, u32[]{:S(2)}) collective-permute-start(f32[1,256,128]{2,1,0:T(8,128)S(1)} %get-tuple-element.270), channel_id=1, source_target_pairs={{0,1},{1,2},{2,3},{3,4},{4,5},{5,6},{6,7},{7,8},{8,9},{9,10},{10,1... | collective-permute-start | bytes 393224 | tf_op jit(solution)/shard_map/while/body/eval_jaxpr/ppermute | solution.py:16
  113.9 9.1 %collective-permute-start.1 = (f32[1,256,128]{2,1,0:T(8,128)S(1)}, f32[1,256,128]{2,1,0:T(8,128)S(1)}, u32[]{:S(2)}, u32[]{:S(2)}) collective-permute-start(f32[1,256,128]{2,1,0:T(8,128)S(1)} %get-tuple-element.271), channel_id=1, source_target_pairs={{1,0},{2,1},{3,2},{4,3},{5,4},{6,5},{7,6},{8,7},{9,8},{10,9},{11,1... | collective-permute-start | bytes 393224 | tf_op jit(solution)/shard_map/while/body/eval_jaxpr/ppermute | solution.py:19
  123.4 9.3 %collective-permute-start = (f32[1,256,128]{2,1,0:T(8,128)S(1)}, f32[1,256,128]{2,1,0:T(8,128)S(1)}, u32[]{:S(2)}, u32[]{:S(2)}) collective-permute-start(f32[1,256,128]{2,1,0:T(8,128)S(1)} %get-tuple-element.270), channel_id=1, source_target_pairs={{0,1},{1,2},{2,3},{3,4},{4,5},{5,6},{6,7},{7,8},{8,9},{9,10},{10,1... | collective-permute-start | bytes 393224 | tf_op jit(solution)/shard_map/while/body/eval_jaxpr/ppermute | solution.py:16
  125.3 9.0 %collective-permute-start.1 = (f32[1,256,128]{2,1,0:T(8,128)S(1)}, f32[1,256,128]{2,1,0:T(8,128)S(1)}, u32[]{:S(2)}, u32[]{:S(2)}) collective-permute-start(f32[1,256,128]{2,1,0:T(8,128)S(1)} %get-tuple-element.271), channel_id=1, source_target_pairs={{1,0},{2,1},{3,2},{4,3},{5,4},{6,5},{7,6},{8,7},{9,8},{10,9},{11,1... | collective-permute-start | bytes 393224 | tf_op jit(solution)/shard_map/while/body/eval_jaxpr/ppermute | solution.py:19
  135.5 280.4 %copy-start.1 = (f32[2,256,128]{2,1,0:T(8,128)S(1)}, f32[2,256,128]{2,1,0:T(8,128)}, u32[]{:S(2)}) copy-start(f32[2,256,128]{2,1,0:T(8,128)} %get-tuple-element.207) | copy-start | bytes 786436
  135.5 280.4 %copy-start.2 = (f32[2,256,128]{2,1,0:T(8,128)S(1)}, f32[2,256,128]{2,1,0:T(8,128)}, u32[]{:S(2)}) copy-start(f32[2,256,128]{2,1,0:T(8,128)} %get-tuple-element.208) | copy-start | bytes 786436
  135.5 261.3 %all-gather.7.cloned.1.call-start = ((), (), s32[]{:S(2)}) async-start(), calls=%async_computation.4 | async-start | bytes 4456448 | tf_op jit(solution)/shard_map/all_gather | solution.py:26
  138.5 278.3 %all-to-all-start.2 = ((f32[16,2,2,4,128]{4,3,2,1,0:T(4,128)}), f32[16,2,2,4,128]{4,3,2,1,0:T(4,128)S(1)}, u32[]{:S(2)}, u32[]{:S(2)}) async-start(f32[16,2,2,4,128]{4,3,2,1,0:T(4,128)} %select_select_fusion), calls=%async_computation.2 | async-start | bytes 262144 | tf_op jit(solution)/shard_map/all_to_all | solution.py:94
  416.8 19.2 %all-to-all-start.1 = ((f32[1,2,256,128]{3,1,0,2:T(2,128)}), f32[1,2,256,128]{3,1,0,2:T(2,128)S(1)}, u32[]{:S(2)}, u32[]{:S(2)}) async-start(f32[1,2,256,128]{3,1,0,2:T(2,128)} %copy.19), calls=%async_computation.1 | async-start | bytes 524288 | tf_op jit(solution)/shard_map/all_to_all | solution.py:102
Sparse Core Ops, SparseCore 0:
  135.6 130.7 all-gather.4
  269.6 127.1 all-gather.6
where the time goes:
time: 445 us; the launch traced here: 444 us
  waiting for transfers between devices  297 us (67%)
  starting transfers between devices  102 us (23%)
  other arithmetic  24.4 us (5%)
  between operations  14.3 us (3%)
  local copies, waits for them, and re-layouts  5.96 us (1%)
    all_gather x2, waiting for transfers between devices, entering(): pieces = jax.tree.map(lambda part: lax.all_gather(part, axis), value)  252 us
    ppermute x9, starting transfers between devices, with_halo(): lax.ppermute(lax.slice_in_dim(block, 0, width, axis=dim), axis, backward)  57.5 us
    select_n x15, other arithmetic, turn(): jnp.where(position < mine, new, old)  18.7 us
    ppermute x9, waiting for transfers between devices, with_halo(): lax.ppermute(lax.slice_in_dim(block, 0, width, axis=dim), axis, backward)  18.5 us
    ppermute x9, starting transfers between devices, with_halo(): lax.ppermute(lax.slice_in_dim(block, block.shape[dim] - width, None, axis...  18.1 us
    all_to_all x1, starting transfers between devices, body(): lax.all_to_all(states, 'cuts', split_axis=0, concat_axis=2, tiled=True)[0]  15.7 us
    all_to_all x1, waiting for transfers between devices, body(): lax.all_to_all(newest[None], 'cuts', split_axis=2, concat_axis=0, tiled=T...  14.8 us
  transfers between devices with their start and end apart: 23, of which 21 were waited for; matrix products, arithmetic and copies ran while one was open for 5% of the time, Pallas kernels for 0%

commit v1 on v0

--- a/solution.py
+++ b/solution.py
@@ -6,6 +6,14 @@
 FINE = 8
 BY = 4
 courant = 0.45
+
+
+def rings_feed(s0):
+    piece_out = lax.axis_size("cuts")
+    v1 = jnp.split(s0, piece_out, axis=0)
+    local_out = jnp.stack(v1, axis=0)
+    val = lax.all_to_all(local_out, "cuts", 0, 0)
+    return jnp.concatenate(val, axis=2)
 
 
 def with_halo(block, sides, width):
@@ -74,7 +82,7 @@
     position = lax.axis_index("cuts")
     layers = diffusivity.shape[0]
     y_rows = diffusivity.shape[1]
-    slice_start = lax.all_to_all(states, "cuts", split_axis=0, concat_axis=2, tiled=True)[0]
+    slice_start = rings_feed(states)[0]
     halo_depth = 1
     kappa_ext = with_halo(diffusivity, (("slab", 0),), halo_depth)
     face_z, face_y, face_x = face_values(kappa_ext)

time: 445 us -> 468 us (1.052)
  local copies, waits for them, and re-layouts: 5.96 us -> 27.1 us
    unnamed x15 -> x30, local copies, waits for them, and re-layouts: 2.42 us -> 22.3 us
  transfers between devices with their start and end apart: 23 -> 23, of which waited for: 21 -> 21; matrix products, arithmetic and copies ran while one was open for 5% -> 10% of each run, Pallas kernels for 0% -> 0%
where the time goes in v1:
time: 468 us; the launch traced here: 465 us
  waiting for transfers between devices  297 us (63%)
  starting transfers between devices  102 us (22%)
  local copies, waits for them, and re-layouts  27.1 us (6%)
  other arithmetic  24.4 us (5%)
  between operations  14.3 us (3%)
    all_gather x2, waiting for transfers between devices, entering(): pieces = jax.tree.map(lambda part: lax.all_gather(part, axis), value)  252 us
    ppermute x9, starting transfers between devices, with_halo(): lax.ppermute(lax.slice_in_dim(block, 0, width, axis=dim), axis, backward)  57.5 us
    unnamed x30, local copies, waits for them, and re-layouts  22.3 us
    select_n x15, other arithmetic, turn(): jnp.where(position < mine, new, old)  18.7 us
    ppermute x9, waiting for transfers between devices, with_halo(): lax.ppermute(lax.slice_in_dim(block, 0, width, axis=dim), axis, backward)  18.5 us
    ppermute x9, starting transfers between devices, with_halo(): lax.ppermute(lax.slice_in_dim(block, block.shape[dim] - width, None, axis...  18.1 us
    all_to_all x1, starting transfers between devices, rings_feed(): val = lax.all_to_all(local_out, 'cuts', 0, 0)  15.6 us
    all_to_all x1, waiting for transfers between devices, body(): lax.all_to_all(newest[None], 'cuts', split_axis=2, concat_axis=0, tiled=T...  14.8 us
  transfers between devices with their start and end apart: 23, of which 21 were waited for; matrix products, arithmetic and copies ran while one was open for 10% of the time, Pallas kernels for 0%

profile of v1, /device:TPU:2, one launch (start us, length us, event | category | flops | bytes accessed | tf_op | source)
XLA Modules:
  0.0 465.4 jit_solution(11347986394968924198)
XLA Ops:
  8.2 1.9 collective-permute-start.3
  10.1 1.3 constant_dynamic-update-slice_fusion.15
  11.4 1.3 constant_dynamic-update-slice_fusion.14
  12.8 1.3 constant_dynamic-update-slice_fusion.13
  14.1 1.3 constant_dynamic-update-slice_fusion.12
  15.4 1.3 constant_dynamic-update-slice_fusion.11
  16.7 1.3 constant_dynamic-update-slice_fusion.10
  18.0 1.3 constant_dynamic-update-slice_fusion.9
  19.4 1.3 constant_dynamic-update-slice_fusion.8
  20.7 1.3 constant_dynamic-update-slice_fusion.7
  22.0 1.3 constant_dynamic-update-slice_fusion.6
  23.3 1.3 constant_dynamic-update-slice_fusion.5
  24.7 1.3 constant_dynamic-update-slice_fusion.4
  26.0 1.3 constant_dynamic-update-slice_fusion.3
  27.3 1.3 constant_dynamic-update-slice_fusion.2
  28.6 1.3 constant_dynamic-update-slice_fusion.1
  30.0 1.3 constant_dynamic-update-slice_fusion
  31.3 15.6 %all-to-all-start = ((f32[16,1,2,16,128]{4,3,2,1,0:T(8,128)}), f32[16,1,2,16,128]{4,3,2,1,0:T(8,128)S(1)}, u32[]{:S(2)}, u32[]{:S(2)}) async-start(f32[16,1,2,16,128]{4,3,2,1,0:T(8,128)} %constant_dynamic-update-slice_fusion), calls=%async_computation | async-start | bytes 524288 | tf_op jit(solution)/shard_map/all_to_all | solution.py:15
  47.0 6.1 %collective-permute-start.2 = (f32[1,256,128]{2,1,0:T(8,128)S(1)}, f32[1,256,128]{2,1,0:T(8,128)S(1)}, u32[]{:S(2)}, u32[]{:S(2)}) collective-permute-start(f32[1,256,128]{2,1,0:T(8,128)S(1)} %get-tuple-element.210), channel_id=1, source_target_pairs={{1,0},{2,1},{3,2},{4,3},{5,4},{6,5},{7,6},{8,7},{9,8},{10,9},{11,1... | collective-permute-start | bytes 393224 | tf_op jit(solution)/shard_map/ppermute | solution.py:27
  54.1 3.4 collective-permute-done.2
  59.0 4.8 %all-to-all-done = f32[16,1,2,16,128]{4,3,2,1,0:T(8,128)S(1)} async-done(((f32[16,1,2,16,128]{4,3,2,1,0:T(8,128)}), f32[16,1,2,16,128]{4,3,2,1,0:T(8,128)S(1)}, u32[]{:S(2)}, u32[]{:S(2)}) %all-to-all-start) | async-done | bytes 262176 | tf_op jit(solution)/shard_map/all_to_all | solution.py:15
  63.9 91.9 %while.26 = (s32[]{:T(128)}, f32[2,256,128]{2,1,0:T(8,128)S(1)}, f32[3,256,128]{2,1,0:T(8,128)S(1)}, f32[4,257,128]{2,1,0:T(8,128)S(1)}, f32[4,256,129]{2,1,0:T(8,128)S(1)}, /*index=5*/s32[]{:T(128)}) while((s32[]{:T(128)}, f32[2,256,128]{2,1,0:T(8,128)S(1)}, f32[3,256,128]{2,1,0:T(8,128)S(1)}, f32[4,257,128]{2,1,0:T(8,128)S(1)}, ...), condition=%wide.region_1.2_spmd, body=%wide.region_0.1_spmd.sunk | while | flops 1507330 | bytes 4456597 | solution.py:94
  63.9 2.7 collective-permute-start
  66.7 5.7 %collective-permute-start.1 = (f32[1,256,128]{2,1,0:T(8,128)S(1)}, f32[1,256,128]{2,1,0:T(8,128)S(1)}, u32[]{:S(2)}, u32[]{:S(2)}) collective-permute-start(f32[1,256,128]{2,1,0:T(8,128)S(1)} %get-tuple-element.271), channel_id=1, source_target_pairs={{1,0},{2,1},{3,2},{4,3},{5,4},{6,5},{7,6},{8,7},{9,8},{10,9},{11,1... | collective-permute-start | bytes 393224 | tf_op jit(solution)/shard_map/while/body/eval_jaxpr/ppermute | solution.py:27
  73.1 1.7 collective-permute-done.1
  75.2 1.9 collective-permute-start
  77.1 6.5 %collective-permute-start.1 = (f32[1,256,128]{2,1,0:T(8,128)S(1)}, f32[1,256,128]{2,1,0:T(8,128)S(1)}, u32[]{:S(2)}, u32[]{:S(2)}) collective-permute-start(f32[1,256,128]{2,1,0:T(8,128)S(1)} %get-tuple-element.271), channel_id=1, source_target_pairs={{1,0},{2,1},{3,2},{4,3},{5,4},{6,5},{7,6},{8,7},{9,8},{10,9},{11,1... | collective-permute-start | bytes 393224 | tf_op jit(solution)/shard_map/while/body/eval_jaxpr/ppermute | solution.py:27
  84.4 1.7 collective-permute-done.1
  86.5 1.9 collective-permute-start
  88.5 6.5 %collective-permute-start.1 = (f32[1,256,128]{2,1,0:T(8,128)S(1)}, f32[1,256,128]{2,1,0:T(8,128)S(1)}, u32[]{:S(2)}, u32[]{:S(2)}) collective-permute-start(f32[1,256,128]{2,1,0:T(8,128)S(1)} %get-tuple-element.271), channel_id=1, source_target_pairs={{1,0},{2,1},{3,2},{4,3},{5,4},{6,5},{7,6},{8,7},{9,8},{10,9},{11,1... | collective-permute-start | bytes 393224 | tf_op jit(solution)/shard_map/while/body/eval_jaxpr/ppermute | solution.py:27
  95.8 2.0 collective-permute-done.1
  98.1 1.9 collective-permute-start
  100.1 6.6 %collective-permute-start.1 = (f32[1,256,128]{2,1,0:T(8,128)S(1)}, f32[1,256,128]{2,1,0:T(8,128)S(1)}, u32[]{:S(2)}, u32[]{:S(2)}) collective-permute-start(f32[1,256,128]{2,1,0:T(8,128)S(1)} %get-tuple-element.271), channel_id=1, source_target_pairs={{1,0},{2,1},{3,2},{4,3},{5,4},{6,5},{7,6},{8,7},{9,8},{10,9},{11,1... | collective-permute-start | bytes 393224 | tf_op jit(solution)/shard_map/while/body/eval_jaxpr/ppermute | solution.py:27
  107.4 1.8 collective-permute-done.1
  109.5 1.9 collective-permute-start
  111.4 6.5 %collective-permute-start.1 = (f32[1,256,128]{2,1,0:T(8,128)S(1)}, f32[1,256,128]{2,1,0:T(8,128)S(1)}, u32[]{:S(2)}, u32[]{:S(2)}) collective-permute-start(f32[1,256,128]{2,1,0:T(8,128)S(1)} %get-tuple-element.271), channel_id=1, source_target_pairs={{1,0},{2,1},{3,2},{4,3},{5,4},{6,5},{7,6},{8,7},{9,8},{10,9},{11,1... | collective-permute-start | bytes 393224 | tf_op jit(solution)/shard_map/while/body/eval_jaxpr/ppermute | solution.py:27
  118.7 2.6 collective-permute-done.1
  121.7 1.9 collective-permute-start
  123.7 6.6 %collective-permute-start.1 = (f32[1,256,128]{2,1,0:T(8,128)S(1)}, f32[1,256,128]{2,1,0:T(8,128)S(1)}, u32[]{:S(2)}, u32[]{:S(2)}) collective-permute-start(f32[1,256,128]{2,1,0:T(8,128)S(1)} %get-tuple-element.271), channel_id=1, source_target_pairs={{1,0},{2,1},{3,2},{4,3},{5,4},{6,5},{7,6},{8,7},{9,8},{10,9},{11,1... | collective-permute-start | bytes 393224 | tf_op jit(solution)/shard_map/while/body/eval_jaxpr/ppermute | solution.py:27
  131.0 1.8 collective-permute-done.1
  133.2 1.9 collective-permute-start
  135.1 6.6 %collective-permute-start.1 = (f32[1,256,128]{2,1,0:T(8,128)S(1)}, f32[1,256,128]{2,1,0:T(8,128)S(1)}, u32[]{:S(2)}, u32[]{:S(2)}) collective-permute-start(f32[1,256,128]{2,1,0:T(8,128)S(1)} %get-tuple-element.271), channel_id=1, source_target_pairs={{1,0},{2,1},{3,2},{4,3},{5,4},{6,5},{7,6},{8,7},{9,8},{10,9},{11,1... | collective-permute-start | bytes 393224 | tf_op jit(solution)/shard_map/while/body/eval_jaxpr/ppermute | solution.py:27
  142.5 1.7 collective-permute-done.1
  144.5 1.9 collective-permute-start
  146.5 6.5 %collective-permute-start.1 = (f32[1,256,128]{2,1,0:T(8,128)S(1)}, f32[1,256,128]{2,1,0:T(8,128)S(1)}, u32[]{:S(2)}, u32[]{:S(2)}) collective-permute-start(f32[1,256,128]{2,1,0:T(8,128)S(1)} %get-tuple-element.271), channel_id=1, source_target_pairs={{1,0},{2,1},{3,2},{4,3},{5,4},{6,5},{7,6},{8,7},{9,8},{10,9},{11,1... | collective-permute-start | bytes 393224 | tf_op jit(solution)/shard_map/while/body/eval_jaxpr/ppermute | solution.py:27
  153.8 1.7 collective-permute-done.1
  159.7 6.1 %all-to-all-start.2 = ((f32[16,2,2,4,128]{4,3,2,1,0:T(4,128)}), f32[16,2,2,4,128]{4,3,2,1,0:T(4,128)S(1)}, u32[]{:S(2)}, u32[]{:S(2)}) async-start(f32[16,2,2,4,128]{4,3,2,1,0:T(4,128)} %select_select_fusion), calls=%async_computation.2 | async-start | bytes 262144 | tf_op jit(solution)/shard_map/all_to_all | solution.py:102
  165.7 121.9 %all-gather.5.cloned.1.call-done = f32[32,256,128]{2,1,0:T(8,128)} async-done(((f32[2,256,128]{2,1,0:T(8,128)}), f32[32,256,128]{2,1,0:T(8,128)}) %all-gather.5.cloned.1.call-update) | async-done | bytes 4194320 | tf_op jit(solution)/shard_map/all_gather | solution.py:34
  287.6 130.4 %all-gather.7.cloned.1.call-done = f32[32,256,128]{2,1,0:T(8,128)} async-done(((f32[2,256,128]{2,1,0:T(8,128)}), f32[32,256,128]{2,1,0:T(8,128)}) %all-gather.7.cloned.1.call-update) | async-done | bytes 4194320 | tf_op jit(solution)/shard_map/all_gather | solution.py:34
  418.0 19.1 %while.27 = (s32[]{:T(128)}, f32[2,256,128]{2,1,0:T(8,128)S(1)}, s32[]{:T(128)}, f32[16,2,256,128]{3,2,1,0:T(8,128)}, f32[16,2,256,128]{3,2,1,0:T(8,128)}, /*index=5*/s32[]{:T(128)}, s32[]{:T(128)}) while((s32[]{:T(128)}, f32[2,256,128]{2,1,0:T(8,128)S(1)}, s32[]{:T(128)}, f32[16,2,256,128]{3,2,1,0:T(8,128)}, ...), condition=%wide.region_3.4_spmd.clone, body=%wide.region_2.3_spmd.clone.sunk | while | flops 262148 | bytes 1048685 | solution.py:43
  419.2 1.2 fusion.28
  420.5 1.2 fusion.28
  421.8 1.2 fusion.28
  423.0 1.2 fusion.28
  424.3 1.2 fusion.28
  425.6 1.2 fusion.28
  426.9 1.2 fusion.28
  428.1 1.2 fusion.28
  429.4 1.2 fusion.28
  430.7 1.2 fusion.28
  432.0 1.2 fusion.28
  433.2 1.2 fusion.28
  438.0 4.4 all-to-all-start.1
  442.4 14.8 %all-to-all-done.1 = f32[1,2,256,128]{3,1,0,2:T(2,128)S(1)} async-done(((f32[1,2,256,128]{3,1,0,2:T(2,128)}), f32[1,2,256,128]{3,1,0,2:T(2,128)S(1)}, u32[]{:S(2)}, u32[]{:S(2)}) %all-to-all-start.1) | async-done | bytes 262176 | tf_op jit(solution)/shard_map/all_to_all | solution.py:110
  (79 shorter events, 22.4 us)
Async XLA Ops:
  7.2 150.3 %copy-start = (s32[16,16,2]{1,2,0:T(2,128)S(1)}, s32[16,16,2]{1,2,0:T(2,128)}, u32[]{:S(2)}) copy-start(s32[16,16,2]{1,2,0:T(2,128)} %param.12) | copy-start | bytes 6148
  8.2 44.9 %collective-permute-start.3 = (f32[1,256,128]{2,1,0:T(8,128)S(1)}, f32[1,256,128]{2,1,0:T(8,128)S(1)}, u32[]{:S(2)}, u32[]{:S(2)}) collective-permute-start(f32[1,256,128]{2,1,0:T(8,128)S(1)} %get-tuple-element.209), channel_id=1, source_target_pairs={{0,1},{1,2},{2,3},{3,4},{4,5},{5,6},{6,7},{7,8},{8,9},{9,10},{10,1... | collective-permute-start | bytes 393224 | tf_op jit(solution)/shard_map/ppermute | solution.py:24
  31.3 32.5 %all-to-all-start = ((f32[16,1,2,16,128]{4,3,2,1,0:T(8,128)}), f32[16,1,2,16,128]{4,3,2,1,0:T(8,128)S(1)}, u32[]{:S(2)}, u32[]{:S(2)}) async-start(f32[16,1,2,16,128]{4,3,2,1,0:T(8,128)} %constant_dynamic-update-slice_fusion), calls=%async_computation | async-start | bytes 524288 | tf_op jit(solution)/shard_map/all_to_all | solution.py:15
  46.9 240.7 %all-gather.5.cloned.1.call-start = ((), (), s32[]{:S(2)}) async-start(), calls=%async_computation.3 | async-start | bytes 4456448 | tf_op jit(solution)/shard_map/all_gather | solution.py:34
  47.0 10.5 %collective-permute-start.2 = (f32[1,256,128]{2,1,0:T(8,128)S(1)}, f32[1,256,128]{2,1,0:T(8,128)S(1)}, u32[]{:S(2)}, u32[]{:S(2)}) collective-permute-start(f32[1,256,128]{2,1,0:T(8,128)S(1)} %get-tuple-element.210), channel_id=1, source_target_pairs={{1,0},{2,1},{3,2},{4,3},{5,4},{6,5},{7,6},{8,7},{9,8},{10,9},{11,1... | collective-permute-start | bytes 393224 | tf_op jit(solution)/shard_map/ppermute | solution.py:27
  63.8 92.0 %copy-start.3 = (f32[2,256,128]{2,1,0:T(8,128)S(1)}, f32[2,256,128]{2,1,0:T(8,128)}, u32[]{:S(2)}) copy-start(f32[2,256,128]{2,1,0:T(8,128)} %param.11) | copy-start | bytes 786436
  63.9 94.1 %copy-start.4 = (s32[16,16]{1,0:T(8,128)S(1)}, s32[16,16]{1,0:T(8,128)}, u32[]{:S(2)}) copy-start(s32[16,16]{1,0:T(8,128)} %param.13) | copy-start | bytes 3076
  63.9 9.2 %collective-permute-start = (f32[1,256,128]{2,1,0:T(8,128)S(1)}, f32[1,256,128]{2,1,0:T(8,128)S(1)}, u32[]{:S(2)}, u32[]{:S(2)}) collective-permute-start(f32[1,256,128]{2,1,0:T(8,128)S(1)} %get-tuple-element.270), channel_id=1, source_target_pairs={{0,1},{1,2},{2,3},{3,4},{4,5},{5,6},{6,7},{7,8},{8,9},{9,10},{10,1... | collective-permute-start | bytes 393224 | tf_op jit(solution)/shard_map/while/body/eval_jaxpr/ppermute | solution.py:24
  66.7 8.2 %collective-permute-start.1 = (f32[1,256,128]{2,1,0:T(8,128)S(1)}, f32[1,256,128]{2,1,0:T(8,128)S(1)}, u32[]{:S(2)}, u32[]{:S(2)}) collective-permute-start(f32[1,256,128]{2,1,0:T(8,128)S(1)} %get-tuple-element.271), channel_id=1, source_target_pairs={{1,0},{2,1},{3,2},{4,3},{5,4},{6,5},{7,6},{8,7},{9,8},{10,9},{11,1... | collective-permute-start | bytes 393224 | tf_op jit(solution)/shard_map/while/body/eval_jaxpr/ppermute | solution.py:27
  75.2 9.2 %collective-permute-start = (f32[1,256,128]{2,1,0:T(8,128)S(1)}, f32[1,256,128]{2,1,0:T(8,128)S(1)}, u32[]{:S(2)}, u32[]{:S(2)}) collective-permute-start(f32[1,256,128]{2,1,0:T(8,128)S(1)} %get-tuple-element.270), channel_id=1, source_target_pairs={{0,1},{1,2},{2,3},{3,4},{4,5},{5,6},{6,7},{7,8},{8,9},{9,10},{10,1... | collective-permute-start | bytes 393224 | tf_op jit(solution)/shard_map/while/body/eval_jaxpr/ppermute | solution.py:24
  77.1 9.0 %collective-permute-start.1 = (f32[1,256,128]{2,1,0:T(8,128)S(1)}, f32[1,256,128]{2,1,0:T(8,128)S(1)}, u32[]{:S(2)}, u32[]{:S(2)}) collective-permute-start(f32[1,256,128]{2,1,0:T(8,128)S(1)} %get-tuple-element.271), channel_id=1, source_target_pairs={{1,0},{2,1},{3,2},{4,3},{5,4},{6,5},{7,6},{8,7},{9,8},{10,9},{11,1... | collective-permute-start | bytes 393224 | tf_op jit(solution)/shard_map/while/body/eval_jaxpr/ppermute | solution.py:27
  86.5 9.3 %collective-permute-start = (f32[1,256,128]{2,1,0:T(8,128)S(1)}, f32[1,256,128]{2,1,0:T(8,128)S(1)}, u32[]{:S(2)}, u32[]{:S(2)}) collective-permute-start(f32[1,256,128]{2,1,0:T(8,128)S(1)} %get-tuple-element.270), channel_id=1, source_target_pairs={{0,1},{1,2},{2,3},{3,4},{4,5},{5,6},{6,7},{7,8},{8,9},{9,10},{10,1... | collective-permute-start | bytes 393224 | tf_op jit(solution)/shard_map/while/body/eval_jaxpr/ppermute | solution.py:24
  88.5 9.3 %collective-permute-start.1 = (f32[1,256,128]{2,1,0:T(8,128)S(1)}, f32[1,256,128]{2,1,0:T(8,128)S(1)}, u32[]{:S(2)}, u32[]{:S(2)}) collective-permute-start(f32[1,256,128]{2,1,0:T(8,128)S(1)} %get-tuple-element.271), channel_id=1, source_target_pairs={{1,0},{2,1},{3,2},{4,3},{5,4},{6,5},{7,6},{8,7},{9,8},{10,9},{11,1... | collective-permute-start | bytes 393224 | tf_op jit(solution)/shard_map/while/body/eval_jaxpr/ppermute | solution.py:27
  98.1 9.2 %collective-permute-start = (f32[1,256,128]{2,1,0:T(8,128)S(1)}, f32[1,256,128]{2,1,0:T(8,128)S(1)}, u32[]{:S(2)}, u32[]{:S(2)}) collective-permute-start(f32[1,256,128]{2,1,0:T(8,128)S(1)} %get-tuple-element.270), channel_id=1, source_target_pairs={{0,1},{1,2},{2,3},{3,4},{4,5},{5,6},{6,7},{7,8},{8,9},{9,10},{10,1... | collective-permute-start | bytes 393224 | tf_op jit(solution)/shard_map/while/body/eval_jaxpr/ppermute | solution.py:24
  100.1 9.1 %collective-permute-start.1 = (f32[1,256,128]{2,1,0:T(8,128)S(1)}, f32[1,256,128]{2,1,0:T(8,128)S(1)}, u32[]{:S(2)}, u32[]{:S(2)}) collective-permute-start(f32[1,256,128]{2,1,0:T(8,128)S(1)} %get-tuple-element.271), channel_id=1, source_target_pairs={{1,0},{2,1},{3,2},{4,3},{5,4},{6,5},{7,6},{8,7},{9,8},{10,9},{11,1... | collective-permute-start | bytes 393224 | tf_op jit(solution)/shard_map/while/body/eval_jaxpr/ppermute | solution.py:27
  109.5 9.2 %collective-permute-start = (f32[1,256,128]{2,1,0:T(8,128)S(1)}, f32[1,256,128]{2,1,0:T(8,128)S(1)}, u32[]{:S(2)}, u32[]{:S(2)}) collective-permute-start(f32[1,256,128]{2,1,0:T(8,128)S(1)} %get-tuple-element.270), channel_id=1, source_target_pairs={{0,1},{1,2},{2,3},{3,4},{4,5},{5,6},{6,7},{7,8},{8,9},{9,10},{10,1... | collective-permute-start | bytes 393224 | tf_op jit(solution)/shard_map/while/body/eval_jaxpr/ppermute | solution.py:24
  111.4 9.9 %collective-permute-start.1 = (f32[1,256,128]{2,1,0:T(8,128)S(1)}, f32[1,256,128]{2,1,0:T(8,128)S(1)}, u32[]{:S(2)}, u32[]{:S(2)}) collective-permute-start(f32[1,256,128]{2,1,0:T(8,128)S(1)} %get-tuple-element.271), channel_id=1, source_target_pairs={{1,0},{2,1},{3,2},{4,3},{5,4},{6,5},{7,6},{8,7},{9,8},{10,9},{11,1... | collective-permute-start | bytes 393224 | tf_op jit(solution)/shard_map/while/body/eval_jaxpr/ppermute | solution.py:27
  121.7 9.3 %collective-permute-start = (f32[1,256,128]{2,1,0:T(8,128)S(1)}, f32[1,256,128]{2,1,0:T(8,128)S(1)}, u32[]{:S(2)}, u32[]{:S(2)}) collective-permute-start(f32[1,256,128]{2,1,0:T(8,128)S(1)} %get-tuple-element.270), channel_id=1, source_target_pairs={{0,1},{1,2},{2,3},{3,4},{4,5},{5,6},{6,7},{7,8},{8,9},{9,10},{10,1... | collective-permute-start | bytes 393224 | tf_op jit(solution)/shard_map/while/body/eval_jaxpr/ppermute | solution.py:24
  123.7 9.1 %collective-permute-start.1 = (f32[1,256,128]{2,1,0:T(8,128)S(1)}, f32[1,256,128]{2,1,0:T(8,128)S(1)}, u32[]{:S(2)}, u32[]{:S(2)}) collective-permute-start(f32[1,256,128]{2,1,0:T(8,128)S(1)} %get-tuple-element.271), channel_id=1, source_target_pairs={{1,0},{2,1},{3,2},{4,3},{5,4},{6,5},{7,6},{8,7},{9,8},{10,9},{11,1... | collective-permute-start | bytes 393224 | tf_op jit(solution)/shard_map/while/body/eval_jaxpr/ppermute | solution.py:27
  133.2 9.3 %collective-permute-start = (f32[1,256,128]{2,1,0:T(8,128)S(1)}, f32[1,256,128]{2,1,0:T(8,128)S(1)}, u32[]{:S(2)}, u32[]{:S(2)}) collective-permute-start(f32[1,256,128]{2,1,0:T(8,128)S(1)} %get-tuple-element.270), channel_id=1, source_target_pairs={{0,1},{1,2},{2,3},{3,4},{4,5},{5,6},{6,7},{7,8},{8,9},{9,10},{10,1... | collective-permute-start | bytes 393224 | tf_op jit(solution)/shard_map/while/body/eval_jaxpr/ppermute | solution.py:24
  135.1 9.1 %collective-permute-start.1 = (f32[1,256,128]{2,1,0:T(8,128)S(1)}, f32[1,256,128]{2,1,0:T(8,128)S(1)}, u32[]{:S(2)}, u32[]{:S(2)}) collective-permute-start(f32[1,256,128]{2,1,0:T(8,128)S(1)} %get-tuple-element.271), channel_id=1, source_target_pairs={{1,0},{2,1},{3,2},{4,3},{5,4},{6,5},{7,6},{8,7},{9,8},{10,9},{11,1... | collective-permute-start | bytes 393224 | tf_op jit(solution)/shard_map/while/body/eval_jaxpr/ppermute | solution.py:27
  144.5 9.3 %collective-permute-start = (f32[1,256,128]{2,1,0:T(8,128)S(1)}, f32[1,256,128]{2,1,0:T(8,128)S(1)}, u32[]{:S(2)}, u32[]{:S(2)}) collective-permute-start(f32[1,256,128]{2,1,0:T(8,128)S(1)} %get-tuple-element.270), channel_id=1, source_target_pairs={{0,1},{1,2},{2,3},{3,4},{4,5},{5,6},{6,7},{7,8},{8,9},{9,10},{10,1... | collective-permute-start | bytes 393224 | tf_op jit(solution)/shard_map/while/body/eval_jaxpr/ppermute | solution.py:24
  146.5 9.0 %collective-permute-start.1 = (f32[1,256,128]{2,1,0:T(8,128)S(1)}, f32[1,256,128]{2,1,0:T(8,128)S(1)}, u32[]{:S(2)}, u32[]{:S(2)}) collective-permute-start(f32[1,256,128]{2,1,0:T(8,128)S(1)} %get-tuple-element.271), channel_id=1, source_target_pairs={{1,0},{2,1},{3,2},{4,3},{5,4},{6,5},{7,6},{8,7},{9,8},{10,9},{11,1... | collective-permute-start | bytes 393224 | tf_op jit(solution)/shard_map/while/body/eval_jaxpr/ppermute | solution.py:27
  156.7 280.4 %copy-start.1 = (f32[2,256,128]{2,1,0:T(8,128)S(1)}, f32[2,256,128]{2,1,0:T(8,128)}, u32[]{:S(2)}) copy-start(f32[2,256,128]{2,1,0:T(8,128)} %get-tuple-element.207) | copy-start | bytes 786436
  156.7 280.4 %copy-start.2 = (f32[2,256,128]{2,1,0:T(8,128)S(1)}, f32[2,256,128]{2,1,0:T(8,128)}, u32[]{:S(2)}) copy-start(f32[2,256,128]{2,1,0:T(8,128)} %get-tuple-element.208) | copy-start | bytes 786436
  156.7 261.3 %all-gather.7.cloned.1.call-start = ((), (), s32[]{:S(2)}) async-start(), calls=%async_computation.4 | async-start | bytes 4456448 | tf_op jit(solution)/shard_map/all_gather | solution.py:34
  159.7 278.3 %all-to-all-start.2 = ((f32[16,2,2,4,128]{4,3,2,1,0:T(4,128)}), f32[16,2,2,4,128]{4,3,2,1,0:T(4,128)S(1)}, u32[]{:S(2)}, u32[]{:S(2)}) async-start(f32[16,2,2,4,128]{4,3,2,1,0:T(4,128)} %select_select_fusion), calls=%async_computation.2 | async-start | bytes 262144 | tf_op jit(solution)/shard_map/all_to_all | solution.py:102
  438.0 19.2 %all-to-all-start.1 = ((f32[1,2,256,128]{3,1,0,2:T(2,128)}), f32[1,2,256,128]{3,1,0,2:T(2,128)S(1)}, u32[]{:S(2)}, u32[]{:S(2)}) async-start(f32[1,2,256,128]{3,1,0,2:T(2,128)} %copy.19), calls=%async_computation.1 | async-start | bytes 524288 | tf_op jit(solution)/shard_map/all_to_all | solution.py:110
Sparse Core Ops, SparseCore 0:
  156.8 130.7 all-gather.4
  290.8 127.1 all-gather.6
